TPU v7x, 32 devices: a whole 2x2x4 slice. The times are simulated.
32 devices in a mesh: dp: 4 (over y, core), owner: 8 (over z, x).
Axes of the slice: x: 2, y: 2, z: 4, core: 2. Of those that a mesh axis runs over, the one named last changes fastest.
Arguments:
- embeddings: bfloat16 [131072, 1024], P(('dp', 'owner')), may hold values from -40 to 40, as said below
- cluster_ids: int32 [131072, 1], P(('dp', 'owner')), may hold values from 0 to 63; in each aligned block of 4096 rows (0 to 4095, 4096 to 8191, ...) at most 128 rows name the same one
- noise: bfloat16 [131072, 256], P(('dp', 'owner')), may hold values from -3 to 3
- start_basis: float32 [1024, 256], replicated, may hold values from -0.1875 to 0.1875
Outputs:
- routed: bfloat16 [4, 64, 8, 128, 256], P('dp', 'owner')
Inputs may be any that keep to these rules, and one draw needn't show every extreme that they name: `embeddings`: entries are of order one around a column mean. `cluster_ids`: no cluster holds more than 128 rows of one device, and some cluster holds exactly 128 rows of some device.
All inputs are finite; a program needn't handle non-finite values.
Results may differ from a plain program's by a relative error of at most 0.0046.
Values may be sent and summed in bfloat16 or wider, within the bound.
No kernel may reach another device: no remote copies, remote signals or barrier semaphores. Data moves between devices by JAX's collectives and lax.ppermute only.
A program may use at most 128 MiB of HBM per device.

v0:
```python
import math
import jax
import jax.numpy as jnp
from jax import lax
from jax.sharding import PartitionSpec as P

CL_DEV = 8


def shards(embeddings, cluster_ids, noise, start_basis):
    highest = lax.Precision.HIGHEST
    rows_dev, feature_width = embeddings.shape
    rank_count = start_basis.shape[1]
    owners = lax.axis_size("owner")
    row_total = rows_dev * lax.axis_size("dp") * owners
    column_sum = jnp.sum(embeddings, axis=0, dtype=jnp.float32)
    second = lax.dot_general(
        embeddings, embeddings, (((0,), (0,)), ((), ())), preferred_element_type=jnp.float32
    )
    second_all, column_all = lax.psum((second, column_sum), ("dp", "owner"))
    mean_vec = column_all / row_total
    covariance = second_all / row_total - jnp.outer(mean_vec, mean_vec)
    image_rows = jnp.dot(covariance, start_basis, precision=highest)
    gram_matrix = jnp.dot(image_rows.T, image_rows, precision=highest)
    lower_factor = jnp.linalg.cholesky(gram_matrix)
    basis_full = lax.linalg.triangular_solve(
        lower_factor, image_rows, left_side=False, lower=True, transpose_a=True
    )
    curved = jnp.dot(covariance, basis_full, precision=highest)
    eigen_vals = jnp.sum(basis_full * curved, axis=0)
    signed = math.sqrt(feature_width) * jnp.sum(basis_full, axis=0)
    flip_sign = signed / jnp.maximum(jnp.abs(signed), 1.0)
    whiten = (basis_full * (flip_sign / jnp.sqrt(eigen_vals + 1e-06))).astype(jnp.bfloat16)
    offset = jnp.dot(mean_vec, whiten.astype(jnp.float32), precision=highest)
    clusters = CL_DEV * owners
    capacity = 2 * rows_dev // clusters
    ids_here = cluster_ids[:, 0]
    onehot = (cluster_ids == jnp.arange(clusters, dtype=jnp.int32)[None, :]).astype(jnp.int32)
    before = jnp.cumsum(onehot, axis=0) - onehot
    slot_index = jnp.sum(before * onehot, axis=1)
    destination = ids_here * capacity + slot_index
    projected = (
        jnp.dot(embeddings, whiten, preferred_element_type=jnp.float32)
        - offset
        + noise.astype(jnp.float32)
    ).astype(jnp.bfloat16)
    packed = (
        jnp.zeros((clusters * capacity, rank_count), jnp.bfloat16).at[destination].set(projected)
    )
    packed = packed.reshape(clusters, 1, capacity, rank_count)
    arrived = lax.all_to_all(packed, "owner", split_axis=0, concat_axis=1, tiled=True)
    return arrived[None]


def solution(mesh):
    return jax.shard_map(
        shards,
        mesh=mesh,
        in_specs=(
            P(("dp", "owner"), None),
            P(("dp", "owner"), None),
            P(("dp", "owner"), None),
            P(),
        ),
        out_specs=P("dp", "owner", None, None, None),
        check_vma=False,
    )
```

profile of v0, /device:TPU:0, one launch (start us, length us, event | category | flops | bytes accessed | tf_op | source)
XLA Modules:
  0.0 376.8 jit_solution(5720101799312781308)
XLA Ops:
  6.5 0.0 copy-start
  6.5 0.0 all-reduce.3.cloned.1.call-start
  6.5 15.1 %fusion.32 = f32[1024,1024]{1,0:T(8,128)} fusion(bf16[4096,1024]{1,0:T(8,128)(2,1)} %param.4), kind=kOutput, calls=%fused_computation.64 | convolution fusion | flops 8589934592 | bytes 12582912 | tf_op jit(solution)/shard_map/dot_general | solution.py:17
  21.6 0.0 copy-start.2
  21.6 0.0 copy-start.4
  21.6 0.0 all-reduce.3.cloned.1.call-update
  21.7 1.6 copy-done.2
  23.2 2.9 copy.20
  26.1 0.0 copy-done.4
  26.1 0.1 fusion.18
  26.3 18.4 %reduce-window.6 = s32[64,32,128]{2,1,0:T(8,128)S(1)} reduce-window(s32[64,32,128]{2,1,0:T(8,128)S(1)} %fusion.18, s32[]{:T(128)} %copy.38), window={size=1x1x128 pad=0_0x0_0x127_0}, to_apply=%region_0.0 | reduce-window | flops 33292288 | bytes 2097156 | tf_op jit(solution)/shard_map/reduce-window
  44.7 0.3 slice.61
  45.1 0.4 copy.25
  45.5 0.2 reduce-window.9
  45.7 4.7 %convert_reduce_fusion = f32[1024]{0:T(1024)S(1)} fusion(bf16[4096,1024]{1,0:T(8,128)(2,1)} %param.4), kind=kLoop, calls=%fused_computation.3 | loop fusion | flops 8387584 | bytes 8392704 | tf_op jit(solution)/shard_map/reduce_sum | solution.py:16
  50.4 42.3 %psum.15 = f32[1024]{0:T(1024)S(1)} all-reduce(f32[1024]{0:T(1024)S(1)} %convert_reduce_fusion), channel_id=1, replica_groups=mesh['dp'=4,'owner'=8] {'dp','owner'}, use_global_device_ids=true, to_apply=%region_5.6 | all-reduce | flops 1024 | bytes 8192 | tf_op jit(solution)/shard_map/psum | solution.py:20
  92.7 0.3 broadcast_add_fusion
  93.0 0.9 fusion.17
  94.0 73.1 %all-reduce.3.cloned.1.call-done = f32[1024,1024]{1,0:T(8,128)} async-done(((f32[1024,1024]{1,0:T(8,128)}), f32[1024,1024]{1,0:T(8,128)}) %all-reduce.3.cloned.1.call-update) | async-done | bytes 4194320 | tf_op jit(solution)/shard_map/psum | solution.py:20
  167.1 0.0 copy-done
  167.1 6.1 %fusion.4 = f32[1024,256]{1,0:T(8,128)S(1)} fusion(f32[1024,256]{1,0:T(8,128)S(1)} %copy-done, f32[1024,1024]{1,0:T(8,128)} %all-reduce.3.cloned.1.call-done, f32[1024]{0:T(1024)S(1)} %broadcast_multiply_fusion), kind=kOutput, calls=%fused_computation.10 | convolution fusion | flops 3224371200 | bytes 6295552 | tf_op jit(solution)/shard_map/dot_general | solution.py:23
  173.2 1.8 fusion.33
  175.0 0.1 copy.18
  175.2 11.7 %cholesky.50 = f32[128,128]{1,0:T(8,128)S(1)} custom-call(f32[128,128]{1,0:T(8,128)S(1)} %cholesky.118), custom_call_target="Cholesky" | custom-call | tf_op jit(solution)/shard_map/jit(cholesky)/cholesky | solution.py:25
  187.0 9.8 %custom-call.14 = f32[1,128,128]{1,2,0:T(8,128)S(1)} custom-call(f32[1,128,128]{2,1,0:T(8,128)S(1)} %get-tuple-element.26), custom_call_target="InvertDiagBlocksLowerTriangular" | custom-call | tf_op jit(solution)/shard_map/jit(cholesky)/cholesky | solution.py:25
  196.8 0.2 constant_dynamic-update-slice_fusion.1
  197.0 0.3 convolution_subtract_fusion.2
  197.3 11.7 %cholesky.105 = f32[128,128]{1,0:T(8,128)S(1)} custom-call(f32[128,128]{1,0:T(8,128)S(1)} %convolution_subtract_fusion.2), custom_call_target="Cholesky" | custom-call | tf_op jit(solution)/shard_map/jit(cholesky)/cholesky | solution.py:25
  209.0 0.7 compare_reduce_fusion
  211.2 0.1 triangular_solve.58
  211.3 4.0 %while.1 = (s32[]{:T(128)}, f32[256,256]{1,0:T(8,128)S(1)}, s32[2,2]{1,0:T(2,128)S(1)}, f32[2,128,128]{2,1,0:T(8,128)S(1)}, s32[]{:T(128)}) while((s32[]{:T(128)}, f32[256,256]{1,0:T(8,128)S(1)}, s32[2,2]{1,0:T(2,128)S(1)}, f32[2,128,128]{2,1,0:T(8,128)S(1)}, s32[]{:T(128)}) %tuple.23), condition=%wide.while_cond, body=%wide.while_body.sunk | while | flops 2 | bytes 131181 | solution.py:26
  211.3 0.6 fusion.49
  211.9 1.4 bitcast_dynamic-update-slice_fusion.2
  213.3 0.6 fusion.49
  213.9 1.4 bitcast_dynamic-update-slice_fusion.2
  215.3 19.7 %custom-call.15 = f32[2,128,128]{1,2,0:T(8,128)S(1)} custom-call(f32[2,128,128]{2,1,0:T(8,128)S(1)} %get-tuple-element.12), custom_call_target="InvertDiagBlocksLowerTriangular" | custom-call | tf_op jit(solution)/shard_map/triangular_solve | solution.py:26
  234.9 0.0 copy-start.1
  235.0 0.6 fusion.20
  235.6 1.0 convolution_subtract_fusion.1
  236.6 0.6 fusion.23
  237.2 0.2 fusion.19
  237.4 0.0 copy-done.1
  237.4 0.0 copy-start.3
  237.4 4.5 %fusion.14 = f32[256]{0:T(256)S(1)} fusion(f32[1024,1024]{1,0:T(8,128)S(1)} %copy-done.1, f32[1024]{0:T(1024)S(1)} %broadcast_multiply_fusion, f32[1024,128]{0,1:T(8,128)S(1)} %fusion.23, f32[1024,128]{0,1:T(8,128)S(1)} %fusion.20), kind=kOutput, calls=%fused_computation.20 | convolution fusion | flops 3225157376 | bytes 5248000 | tf_op jit(solution)/shard_map/dot_general | solution.py:29
  241.9 0.1 multiply_convert_fusion
  242.0 0.5 fusion.34
  242.5 0.0 copy-done.3
  242.5 5.8 %fusion.2 = bf16[4096,256]{0,1:T(8,128)(2,1)S(1)} fusion(bf16[1024,256]{0,1:T(8,128)(2,1)S(1)} %multiply_convert_fusion, bf16[4096,1024]{1,0:T(8,128)(2,1)} %param.4, bf16[4096,256]{0,1:T(8,128)(2,1)S(1)} %copy-done.3, f32[256]{0:T(256)S(1)} %bitcast.90), kind=kOutput, calls=%fused_computation.7 | convolution fusion | flops 2151677952 | bytes 13108224 | tf_op jit(solution)/shard_map/dot_general | solution.py:43
  248.3 2.7 copy.21
  251.0 20.9 %scatter_custom_fusion = bf16[8192,256]{1,0:T(8,128)(2,1)} fusion(s32[4096]{0:T(1024)S(1)} %bitcast.89, bf16[4096,256]{1,0:T(8,128)(2,1)} %copy.21, bf16[]{:T(256)} %constant.88.clone.1), kind=kCustom, calls=%fused_computation.17 | custom fusion | bytes 4194816 | tf_op jit(solution)/shard_map/scatter | solution.py:48
  272.0 95.5 %all_to_all.15 = bf16[64,1,128,256]{3,2,1,0:T(8,128)(2,1)S(1)} all-to-all(bf16[64,1,128,256]{3,2,1,0:T(8,128)(2,1)} %bitcast.80), channel_id=1, replica_groups=mesh['dp'=4,'owner'=8] {'owner'}, dimensions={0} | all-to-all | bytes 8388608 | tf_op jit(solution)/shard_map/all_to_all | solution.py:51
  367.5 2.3 copy.23
  (13 shorter events, 0.2 us)
Async XLA Ops:
  6.5 160.6 %copy-start = (f32[1024,256]{1,0:T(8,128)S(1)}, f32[1024,256]{1,0:T(8,128)}, u32[]{:S(2)}) copy-start(f32[1024,256]{1,0:T(8,128)} %param.7) | copy-start | bytes 3145732
  6.5 160.6 %all-reduce.3.cloned.1.call-start = ((), (), s32[]{:S(2)}) async-start(), calls=%async_computation.1 | async-start | bytes 8388608 | tf_op jit(solution)/shard_map/psum | solution.py:20
  21.6 1.6 copy-start.2
  21.6 4.5 %copy-start.4 = (s32[4096,1]{0,1:T(1,128)S(1)}, s32[4096,1]{0,1:T(1,128)}, u32[]{:S(2)}) copy-start(s32[4096,1]{0,1:T(1,128)} %param.5) | copy-start | bytes 49156
  234.9 2.4 copy-start.1
  237.4 5.1 %copy-start.3 = (bf16[4096,256]{0,1:T(8,128)(2,1)S(1)}, bf16[4096,256]{0,1:T(8,128)(2,1)}, u32[]{:S(2)}) copy-start(bf16[4096,256]{0,1:T(8,128)(2,1)} %copy.20) | copy-start | bytes 6291460
Sparse Core Ops, SparseCore 0:
  21.8 145.2 all-reduce.2
where the time goes:
time: 385 us; the launch traced here: 377 us
  blocking collectives  138 us (36%)
  other arithmetic  78.7 us (20%)
  waiting for transfers between devices  73.2 us (19%)
  matrix products  36.5 us (9%)
  local copies, waits for them, and re-layouts  35.3 us (9%)
  between operations  15.3 us (4%)
    all_to_all x1, blocking collectives, shards(): lax.all_to_all(packed, 'owner', split_axis=0, concat_axis=1, tiled=True)  95.5 us
    psum x1, waiting for transfers between devices, shards(): second_all, column_all = lax.psum((second, column_sum), ('dp', 'owner'))  73.1 us
    psum x1, blocking collectives, shards(): second_all, column_all = lax.psum((second, column_sum), ('dp', 'owner'))  42.3 us
    another operation x6, other arithmetic, shards(): lower_factor = jnp.linalg.cholesky(gram_matrix)  34 us
    scatter x1, local copies, waits for them, and re-layouts, shards(): jnp.zeros((clusters * capacity, rank_count), jnp.bfloat16).at[destination]  20.9 us
    another operation x3, other arithmetic, shards(): lax.linalg.triangular_solve(lower_factor, image_rows, left_side=False, lo...  19.7 us
    another operation x3, other arithmetic  19 us
    dot_general x1, matrix products, shards(): lax.dot_general(embeddings, embeddings, (((0,), (0,)), ((), ())), preferr...  15.1 us
  transfers between devices with their start and end apart: 1, of which 1 were waited for; matrix products, arithmetic and copies ran while one was open for 8% of the time, Pallas kernels for 0%

commit v1 on v0

--- a/solution.py
+++ b/solution.py
@@ -5,6 +5,12 @@
 from jax.sharding import PartitionSpec as P
 
 CL_DEV = 8
+
+
+def number_the_runs(target, bus_axis, axis_key):
+    for tick in (bus_axis, axis_key):
+        target = lax.psum(target, axis_name=tick)
+    return target
 
 
 def shards(embeddings, cluster_ids, noise, start_basis):
@@ -17,7 +23,7 @@
     second = lax.dot_general(
         embeddings, embeddings, (((0,), (0,)), ((), ())), preferred_element_type=jnp.float32
     )
-    second_all, column_all = lax.psum((second, column_sum), ("dp", "owner"))
+    second_all, column_all = number_the_runs((second, column_sum), "dp", "owner")
     mean_vec = column_all / row_total
     covariance = second_all / row_total - jnp.outer(mean_vec, mean_vec)
     image_rows = jnp.dot(covariance, start_basis, precision=highest)

time: 385 us -> 489 us (1.27)
  waiting for transfers between devices: 73.2 us -> 192 us
  blocking collectives: 138 us -> 126 us
    psum x1 -> x2, waiting for transfers between devices: 73.1 us -> 192 us  [number_the_runs(): target = lax.psum(target, axis_name=tick)]
    psum x1 -> x2, blocking collectives: 42.3 us -> 28.8 us  [number_the_runs(): target = lax.psum(target, axis_name=tick)]
  transfers between devices with their start and end apart: 1 -> 2, of which waited for: 1 -> 2; matrix products, arithmetic and copies ran while one was open for 8% -> 6% of each run, Pallas kernels for 0% -> 0%
where the time goes in v1:
time: 489 us; the launch traced here: 482 us
  waiting for transfers between devices  192 us (39%)
  blocking collectives  126 us (26%)
  other arithmetic  78.7 us (16%)
  matrix products  36.5 us (7%)
  local copies, waits for them, and re-layouts  33.6 us (7%)
  between operations  15.2 us (3%)
    psum x2, waiting for transfers between devices, number_the_runs(): target = lax.psum(target, axis_name=tick)  192 us
    all_to_all x1, blocking collectives, shards(): lax.all_to_all(packed, 'owner', split_axis=0, concat_axis=1, tiled=True)  96.9 us
    another operation x6, other arithmetic, shards(): lower_factor = jnp.linalg.cholesky(gram_matrix)  34 us
    psum x2, blocking collectives, number_the_runs(): target = lax.psum(target, axis_name=tick)  28.8 us
    scatter x1, local copies, waits for them, and re-layouts, shards(): jnp.zeros((clusters * capacity, rank_count), jnp.bfloat16).at[destination]  20.9 us
    another operation x3, other arithmetic, shards(): lax.linalg.triangular_solve(lower_factor, image_rows, left_side=False, lo...  19.7 us
    another operation x3, other arithmetic  19 us
    dot_general x1, matrix products, shards(): lax.dot_general(embeddings, embeddings, (((0,), (0,)), ((), ())), preferr...  15.1 us
  transfers between devices with their start and end apart: 2, of which 2 were waited for; matrix products, arithmetic and copies ran while one was open for 6% of the time, Pallas kernels for 0%

profile of v1, /device:TPU:0, one launch (start us, length us, event | category | flops | bytes accessed | tf_op | source)
XLA Modules:
  0.0 481.5 jit_solution(6318980991816182094)
XLA Ops:
  6.5 0.0 copy-start
  6.5 0.0 all-reduce.4.cloned.1.call-start
  6.5 15.1 %fusion.32 = f32[1024,1024]{1,0:T(8,128)} fusion(bf16[4096,1024]{1,0:T(8,128)(2,1)} %param.4), kind=kOutput, calls=%fused_computation.64 | convolution fusion | flops 8589934592 | bytes 12582912 | tf_op jit(solution)/shard_map/dot_general | solution.py:23
  21.6 0.0 copy-start.2
  21.6 0.0 all-reduce.4.cloned.1.call-update
  21.7 0.0 all-reduce.6.cloned.1.call-start
  21.7 88.3 %all-reduce.4.cloned.1.call-done = f32[1024,1024]{1,0:T(8,128)} async-done(((f32[1024,1024]{1,0:T(8,128)}), f32[1024,1024]{1,0:T(8,128)}) %all-reduce.4.cloned.1.call-update) | async-done | bytes 4194320 | tf_op jit(solution)/shard_map/psum | solution.py:12
  110.0 0.0 copy-start.4
  110.0 0.0 all-reduce.6.cloned.1.call-update
  110.1 0.0 copy-done.2
  110.1 2.9 copy.20
  112.9 0.0 copy-done.4
  112.9 0.1 fusion.18
  113.1 18.4 %reduce-window.6 = s32[64,32,128]{2,1,0:T(8,128)S(1)} reduce-window(s32[64,32,128]{2,1,0:T(8,128)S(1)} %fusion.18, s32[]{:T(128)} %copy.39), window={size=1x1x128 pad=0_0x0_0x127_0}, to_apply=%region_0.0 | reduce-window | flops 33292288 | bytes 2097156 | tf_op jit(solution)/shard_map/reduce-window
  131.5 0.3 slice.61
  131.9 0.4 copy.25
  132.3 0.2 reduce-window.9
  132.5 4.6 convert_reduce_fusion
  137.1 6.1 %psum.30 = f32[1024]{0:T(1024)S(1)} all-reduce(f32[1024]{0:T(1024)S(1)} %convert_reduce_fusion), channel_id=1, replica_groups=mesh['dp'=4,'owner'=8] {'dp'}, use_global_device_ids=true, to_apply=%region_6.7 | all-reduce | flops 1024 | bytes 8192 | tf_op jit(solution)/shard_map/psum | solution.py:12
  143.3 22.6 %psum.31 = f32[1024]{0:T(1024)S(1)} all-reduce(f32[1024]{0:T(1024)S(1)} %psum.30), channel_id=1, replica_groups=mesh['dp'=4,'owner'=8] {'owner'}, use_global_device_ids=true, to_apply=%region_7.8 | all-reduce | flops 1024 | bytes 8192 | tf_op jit(solution)/shard_map/psum | solution.py:12
  165.9 0.3 broadcast_add_fusion
  166.2 0.9 fusion.17
  167.2 103.4 %all-reduce.6.cloned.1.call-done = f32[1024,1024]{1,0:T(8,128)} async-done(((f32[1024,1024]{1,0:T(8,128)}), f32[1024,1024]{1,0:T(8,128)}) %all-reduce.6.cloned.1.call-update) | async-done | bytes 4194320 | tf_op jit(solution)/shard_map/psum | solution.py:12
  270.6 0.0 copy-done
  270.6 6.1 %fusion.4 = f32[1024,256]{1,0:T(8,128)S(1)} fusion(f32[1024,256]{1,0:T(8,128)S(1)} %copy-done, f32[1024,1024]{1,0:T(8,128)} %all-reduce.6.cloned.1.call-done, f32[1024]{0:T(1024)S(1)} %broadcast_multiply_fusion), kind=kOutput, calls=%fused_computation.10 | convolution fusion | flops 3224371200 | bytes 6295552 | tf_op jit(solution)/shard_map/dot_general | solution.py:29
  276.7 1.8 fusion.33
  278.5 0.1 copy.18
  278.7 11.7 %cholesky.50 = f32[128,128]{1,0:T(8,128)S(1)} custom-call(f32[128,128]{1,0:T(8,128)S(1)} %cholesky.118), custom_call_target="Cholesky" | custom-call | tf_op jit(solution)/shard_map/jit(cholesky)/cholesky | solution.py:31
  290.5 9.8 %custom-call.14 = f32[1,128,128]{1,2,0:T(8,128)S(1)} custom-call(f32[1,128,128]{2,1,0:T(8,128)S(1)} %get-tuple-element.26), custom_call_target="InvertDiagBlocksLowerTriangular" | custom-call | tf_op jit(solution)/shard_map/jit(cholesky)/cholesky | solution.py:31
  300.3 0.2 constant_dynamic-update-slice_fusion.1
  300.5 0.3 convolution_subtract_fusion.2
  300.8 11.7 %cholesky.105 = f32[128,128]{1,0:T(8,128)S(1)} custom-call(f32[128,128]{1,0:T(8,128)S(1)} %convolution_subtract_fusion.2), custom_call_target="Cholesky" | custom-call | tf_op jit(solution)/shard_map/jit(cholesky)/cholesky | solution.py:31
  312.6 0.7 compare_reduce_fusion
  314.7 0.1 triangular_solve.58
  314.7 3.9 while.1
  314.7 0.6 fusion.49
  315.3 1.3 bitcast_dynamic-update-slice_fusion.2
  316.7 0.6 fusion.49
  317.3 1.3 bitcast_dynamic-update-slice_fusion.2
  318.6 19.7 %custom-call.15 = f32[2,128,128]{1,2,0:T(8,128)S(1)} custom-call(f32[2,128,128]{2,1,0:T(8,128)S(1)} %get-tuple-element.12), custom_call_target="InvertDiagBlocksLowerTriangular" | custom-call | tf_op jit(solution)/shard_map/triangular_solve | solution.py:32
  338.3 0.0 copy-start.1
  338.3 0.6 fusion.20
  338.9 1.0 convolution_subtract_fusion.1
  339.9 0.6 fusion.23
  340.6 0.2 fusion.19
  340.7 0.0 copy-done.1
  340.7 0.0 copy-start.3
  340.7 4.5 fusion.14
  345.2 0.1 multiply_convert_fusion
  345.4 0.5 fusion.34
  345.9 0.0 copy-done.3
  345.9 5.8 %fusion.2 = bf16[4096,256]{0,1:T(8,128)(2,1)S(1)} fusion(bf16[1024,256]{0,1:T(8,128)(2,1)S(1)} %multiply_convert_fusion, bf16[4096,1024]{1,0:T(8,128)(2,1)} %param.4, bf16[4096,256]{0,1:T(8,128)(2,1)S(1)} %copy-done.3, f32[256]{0:T(256)S(1)} %bitcast.90), kind=kOutput, calls=%fused_computation.7 | convolution fusion | flops 2151677952 | bytes 13108224 | tf_op jit(solution)/shard_map/dot_general | solution.py:49
  351.7 2.7 copy.21
  354.4 20.9 %scatter_custom_fusion = bf16[8192,256]{1,0:T(8,128)(2,1)} fusion(s32[4096]{0:T(1024)S(1)} %bitcast.89, bf16[4096,256]{1,0:T(8,128)(2,1)} %copy.21, bf16[]{:T(256)} %constant.88.clone.1), kind=kCustom, calls=%fused_computation.17 | custom fusion | bytes 4194816 | tf_op jit(solution)/shard_map/scatter | solution.py:54
  375.3 96.9 %all_to_all.15 = bf16[64,1,128,256]{3,2,1,0:T(8,128)(2,1)S(1)} all-to-all(bf16[64,1,128,256]{3,2,1,0:T(8,128)(2,1)} %bitcast.80), channel_id=1, replica_groups=mesh['dp'=4,'owner'=8] {'owner'}, dimensions={0} | all-to-all | bytes 8388608 | tf_op jit(solution)/shard_map/all_to_all | solution.py:57
  472.2 2.3 copy.23
  (13 shorter events, 0.2 us)
Async XLA Ops:
  6.5 264.1 %copy-start = (f32[1024,256]{1,0:T(8,128)S(1)}, f32[1024,256]{1,0:T(8,128)}, u32[]{:S(2)}) copy-start(f32[1024,256]{1,0:T(8,128)} %param.7) | copy-start | bytes 3145732
  6.5 103.5 %all-reduce.4.cloned.1.call-start = ((), (), s32[]{:S(2)}) async-start(), calls=%async_computation.1 | async-start | bytes 8388608 | tf_op jit(solution)/shard_map/psum | solution.py:12
  21.6 88.4 %copy-start.2 = (bf16[4096,256]{1,0:T(8,128)(2,1)S(1)}, bf16[4096,256]{1,0:T(8,128)(2,1)}, u32[]{:S(2)}) copy-start(bf16[4096,256]{1,0:T(8,128)(2,1)} %param.6) | copy-start | bytes 6291460
  21.7 248.9 %all-reduce.6.cloned.1.call-start = ((), (), s32[]{:S(2)}) async-start(), calls=%async_computation.2 | async-start | bytes 8388608 | tf_op jit(solution)/shard_map/psum | solution.py:12
  110.0 2.9 copy-start.4
  338.3 2.4 copy-start.1
  340.7 5.1 %copy-start.3 = (bf16[4096,256]{0,1:T(8,128)(2,1)S(1)}, bf16[4096,256]{0,1:T(8,128)(2,1)}, u32[]{:S(2)}) copy-start(bf16[4096,256]{0,1:T(8,128)(2,1)} %copy.20) | copy-start | bytes 6291460
Sparse Core Ops, SparseCore 0:
  21.8 88.1 all-reduce.3
  113.7 156.8 all-reduce.5
